TPU v7x, 128 devices: a whole 4x4x4 slice. The times are simulated.
128 devices in a mesh: wide: 16 (over y_lo, z, core), narrow: 8 (over x, y_hi).
Axes of the slice: x: 4, y: 4 (y_hi: 2, y_lo: 2; y = y_hi * 2 + y_lo), z: 4, core: 2. Of those that a mesh axis runs over, the one named last changes fastest.
Arguments:
- fields: float32 [5, 16, 64, 256], P(None, 'wide', 'narrow'), may hold values from -2.1 to 6.1, as said below
- prior_modes: bfloat16 [124, 5, 16, 16384], P(None, None, 'wide', 'narrow'), may hold values from -360 to 360, as said below
Outputs:
- flow_state: float32 [5, 16, 64, 256], P(None, 'wide', 'narrow')
- factor: float32 [128, 128], replicated
Inputs may be any that keep to these rules, and one draw needn't show every extreme that they name: `fields`: density and pressure lie in 0.6 to 1.4, each velocity component below 1.5 in magnitude. `prior_modes`: the columns are linearly independent.
All inputs are finite; a program needn't handle non-finite values.
Results may differ from a plain program's by a relative error of at most 0.0014.
Values may be sent and summed in bfloat16 or wider, within the bound.
No kernel may reach another device: no remote copies, remote signals or barrier semaphores. Data moves between devices by JAX's collectives and lax.ppermute only.
A program may use at most 64 MiB of HBM per device.

v0:
```python
import jax
import jax.numpy as jnp
from jax import lax
from jax.sharding import PartitionSpec as P

STEPS = 2
GAMMA = 1.4
TIME_STEP = 0.25
VISCOSITY = 0.15


def extended(block, sides, width):
    for axis, dim in sides:
        count = lax.axis_size(axis)
        forward = [(i, i + 1) for i in range(count - 1)]
        forward.append((count - 1, 0))
        backward = [(target, source) for source, target in forward]
        low = lax.ppermute(
            lax.slice_in_dim(block, block.shape[dim] - width, None, axis=dim), axis, forward
        )
        high = lax.ppermute(lax.slice_in_dim(block, 0, width, axis=dim), axis, backward)
        block = jnp.concatenate([low, block, high], axis=dim)
    return block


def flux_of(current, dim_index):
    density = current[0]
    momentum = current[1:4]
    energy = current[4]
    vel_d = momentum[dim_index] / density
    pressure = (GAMMA - 1.0) * (
        energy
        - 0.5
        * (momentum[0] * momentum[0] + momentum[1] * momentum[1] + momentum[2] * momentum[2])
        / density
    )
    components = [
        momentum[dim_index],
        momentum[0] * vel_d,
        momentum[1] * vel_d,
        momentum[2] * vel_d,
        (energy + pressure) * vel_d,
    ]
    components[1 + dim_index] = components[1 + dim_index] + pressure
    return jnp.stack(components)


def tendency(current):
    padded = extended(current.astype(jnp.bfloat16), (("wide", 1), ("narrow", 2)), 1).astype(
        current.dtype
    )
    flux_x = flux_of(padded[:, :, 1:-1], 0)
    flux_y = flux_of(padded[:, 1:-1, :], 1)
    flux_z = flux_of(current, 2)
    divergence = (
        flux_x[:, 2:]
        - flux_x[:, :-2]
        + (flux_y[:, :, 2:] - flux_y[:, :, :-2])
        + (jnp.roll(flux_z, -1, 3) - jnp.roll(flux_z, 1, 3))
    )
    laplace = (
        padded[:, 2:, 1:-1]
        + padded[:, :-2, 1:-1]
        + padded[:, 1:-1, 2:]
        + padded[:, 1:-1, :-2]
        + jnp.roll(current, -1, 3)
        + jnp.roll(current, 1, 3)
        - 6.0 * current
    )
    return -0.5 * divergence + VISCOSITY * laplace


def local(fields, prior_modes):
    wide_count = lax.axis_size("wide")
    narrow_count = lax.axis_size("narrow")
    cells_x, cells_y, cells_z = (fields.shape[1], fields.shape[2], fields.shape[3])
    inverse_cells = 1.0 / (cells_x * wide_count * cells_y * narrow_count * cells_z)
    flat_modes = prior_modes.reshape(prior_modes.shape[0], -1)
    contract = (((1,), (1,)), ((), ()))
    gram_modes = lax.dot_general(
        flat_modes, flat_modes, contract, preferred_element_type=jnp.float32
    )
    current = fields
    snapshots = []
    for step_index in range(STEPS):
        section_one = current + TIME_STEP * tendency(current)
        snapshots.append(section_one.astype(jnp.bfloat16))
        current = 0.5 * current + 0.5 * (section_one + TIME_STEP * tendency(section_one))
        snapshots.append(current.astype(jnp.bfloat16))
    arrived = lax.all_to_all(
        jnp.stack(snapshots), "narrow", split_axis=4, concat_axis=3, tiled=True
    )
    snap_rows = jnp.swapaxes(arrived, 3, 4).reshape(arrived.shape[0], -1)
    cross_gram = lax.dot_general(
        flat_modes, snap_rows, contract, preferred_element_type=jnp.float32
    )
    snap_gram = lax.dot_general(snap_rows, snap_rows, contract, preferred_element_type=jnp.float32)
    gram_local = jnp.concatenate(
        [
            jnp.concatenate([gram_modes, cross_gram], 1),
            jnp.concatenate([cross_gram.T, snap_gram], 1),
        ],
        0,
    )
    gram_local = gram_local * inverse_cells
    gram_whole = lax.psum(gram_local, ("wide", "narrow"))
    factor = jnp.linalg.cholesky(gram_whole).T
    return (current, factor)


def solution(mesh):
    placed = (P(None, "wide", "narrow", None), P(None, None, "wide", "narrow"))
    return jax.shard_map(
        local,
        mesh=mesh,
        in_specs=placed,
        out_specs=(P(None, "wide", "narrow", None), P()),
        check_vma=False,
    )
```

profile of v0, /device:TPU:1, one launch (start us, length us, event | category | flops | bytes accessed | tf_op | source)
XLA Modules:
  0.0 256.1 jit_solution(13830206497082720852)
XLA Ops:
  7.2 0.8 convert_element_type.30
  7.9 1.4 collective-permute-start.1
  9.3 1.6 collective-permute-start
  11.0 0.7 constant_dynamic-update-slice_fusion.14
  11.7 0.8 constant_dynamic-update-slice_fusion.13
  12.4 0.7 constant_dynamic-update-slice_fusion.12
  13.1 0.8 constant_dynamic-update-slice_fusion.11
  13.9 0.7 constant_dynamic-update-slice_fusion.10
  14.6 0.9 fusion.98
  15.7 5.2 %collective-permute-start.3 = (bf16[5,3,1,256]{3,1,2,0:T(4,128)(2,1)S(1)}, bf16[5,3,1,256]{3,1,2,0:T(4,128)(2,1)S(1)}, u32[]{:S(2)}, u32[]{:S(2)}) collective-permute-start(bf16[5,3,1,256]{3,1,2,0:T(4,128)(2,1)S(1)} %copy.427), channel_id=1, source_target_pairs={{1,0},{2,1},{3,2},{4,3},{5,4},{6,5},{7,6},{0,7},{9,8},{10,9},{11,1... | collective-permute-start | bytes 23048 | tf_op jit(solution)/shard_map/ppermute | solution.py:21
  20.8 0.8 fusion.99
  21.7 5.3 %collective-permute-done.2 = bf16[5,3,1,256]{3,1,2,0:T(4,128)(2,1)S(1)} collective-permute-done((bf16[5,3,1,256]{3,1,2,0:T(4,128)(2,1)S(1)}, bf16[5,3,1,256]{3,1,2,0:T(4,128)(2,1)S(1)}, u32[]{:S(2)}, u32[]{:S(2)}) %collective-permute-start.2) | collective-permute-done | bytes 7712 | tf_op jit(solution)/shard_map/ppermute | solution.py:18
  27.3 0.9 fusion.83
  28.2 4.9 %collective-permute-start.5 = (bf16[5,1,8,256]{3,2,0,1:T(8,128)(2,1)S(1)}, bf16[5,1,8,256]{3,2,0,1:T(8,128)(2,1)S(1)}, u32[]{:S(2)}, u32[]{:S(2)}) collective-permute-start(bf16[5,1,8,256]{3,2,0,1:T(8,128)(2,1)S(1)} %get-tuple-element.65), channel_id=1, source_target_pairs={{8,0},{16,8},{24,16},{32,24},{40,32},{48,40},{56,48},{64,56},{72,6... | collective-permute-start | bytes 61448 | tf_op jit(solution)/shard_map/ppermute | solution.py:21
  33.0 0.1 fusion.96
  33.2 0.1 fusion.94
  33.3 0.6 collective-permute-done.5
  33.9 1.0 collective-permute-done.4
  34.9 0.7 collective-permute-start.7
  35.6 2.3 collective-permute-start.6
  38.0 1.1 collective-permute-done.7
  39.1 2.6 %collective-permute-done.6 = bf16[5,3,1,256]{3,1,2,0:T(4,128)(2,1)S(1)} collective-permute-done((bf16[5,3,1,256]{3,1,2,0:T(4,128)(2,1)S(1)}, bf16[5,3,1,256]{3,1,2,0:T(4,128)(2,1)S(1)}, u32[]{:S(2)}, u32[]{:S(2)}) %collective-permute-start.6) | collective-permute-done | bytes 7712 | tf_op jit(solution)/shard_map/ppermute | solution.py:18
  42.1 0.1 broadcast_multiply_fusion
  42.2 0.1 fusion.92
  42.3 6.1 %collective-permute-start.9 = (bf16[5,1,8,256]{3,2,0,1:T(8,128)(2,1)S(1)}, bf16[5,1,8,256]{3,2,0,1:T(8,128)(2,1)S(1)}, u32[]{:S(2)}, u32[]{:S(2)}) collective-permute-start(bf16[5,1,8,256]{3,2,0,1:T(8,128)(2,1)S(1)} %fusion.78), channel_id=1, source_target_pairs={{8,0},{16,8},{24,16},{32,24},{40,32},{48,40},{56,48},{64,56},{72,6... | collective-permute-start | bytes 61448 | tf_op jit(solution)/shard_map/ppermute | solution.py:21
  48.5 0.1 fusion.90
  48.7 0.6 collective-permute-done.9
  49.3 0.3 collective-permute-done.8
  49.7 0.1 collective-permute-start.11
  49.8 2.9 %collective-permute-start.10 = (bf16[5,3,1,256]{3,1,2,0:T(4,128)(2,1)S(1)}, bf16[5,3,1,256]{3,1,2,0:T(4,128)(2,1)S(1)}, u32[]{:S(2)}, u32[]{:S(2)}) collective-permute-start(bf16[5,3,1,256]{3,1,2,0:T(4,128)(2,1)S(1)} %copy.394), channel_id=1, source_target_pairs={{0,1},{1,2},{2,3},{3,4},{4,5},{5,6},{6,7},{7,0},{8,9},{9,10},{10,1... | collective-permute-start | bytes 23048 | tf_op jit(solution)/shard_map/ppermute | solution.py:18
  52.8 1.0 collective-permute-done.11
  53.8 2.2 collective-permute-done.10
  56.3 0.1 fusion.80
  56.4 5.4 %collective-permute-start.13 = (bf16[5,1,8,256]{3,2,0,1:T(8,128)(2,1)S(1)}, bf16[5,1,8,256]{3,2,0,1:T(8,128)(2,1)S(1)}, u32[]{:S(2)}, u32[]{:S(2)}) collective-permute-start(bf16[5,1,8,256]{3,2,0,1:T(8,128)(2,1)S(1)} %get-tuple-element.31), channel_id=1, source_target_pairs={{8,0},{16,8},{24,16},{32,24},{40,32},{48,40},{56,48},{64,56},{72,6... | collective-permute-start | bytes 61448 | tf_op jit(solution)/shard_map/ppermute | solution.py:21
  62.0 0.1 fusion.86
  62.2 0.6 collective-permute-done.13
  62.7 0.3 collective-permute-done.12
  63.1 0.1 collective-permute-start.15
  63.2 2.9 %collective-permute-start.14 = (bf16[5,3,1,256]{3,1,2,0:T(4,128)(2,1)S(1)}, bf16[5,3,1,256]{3,1,2,0:T(4,128)(2,1)S(1)}, u32[]{:S(2)}, u32[]{:S(2)}) collective-permute-start(bf16[5,3,1,256]{3,1,2,0:T(4,128)(2,1)S(1)} %copy.405), channel_id=1, source_target_pairs={{0,1},{1,2},{2,3},{3,4},{4,5},{5,6},{6,7},{7,0},{8,9},{9,10},{10,1... | collective-permute-start | bytes 23048 | tf_op jit(solution)/shard_map/ppermute | solution.py:18
  66.2 1.0 collective-permute-done.15
  67.2 2.2 collective-permute-done.14
  69.7 0.7 convert_bitcast_fusion
  70.5 0.7 copy.416
  71.2 2.1 reshape.630
  73.3 3.4 %all-to-all-start = ((bf16[8,2,2560]{2,1,0:T(2,128)(2,1)}), bf16[8,2,2560]{2,1,0:T(2,128)(2,1)S(1)}, u32[]{:S(2)}, u32[]{:S(2)}) async-start(bf16[8,2,2560]{2,1,0:T(2,128)(2,1)} %reshape.630), calls=%async_computation | async-start | bytes 163840 | tf_op jit(solution)/shard_map/all_to_all | solution.py:90
  76.6 0.2 all-reduce.2.cloned.1.call-start
  76.9 3.4 %fusion.2 = f32[124,124]{0,1:T(8,128)S(1)} fusion(bf16[124,5,1,2048]{3,0,2,1:T(8,128)(2,1)} %param.3), kind=kOutput, calls=%fused_computation.2 | convolution fusion | flops 314900480 | bytes 2601024 | tf_op jit(solution)/shard_map/dot_general | solution.py:80
  80.2 3.3 %copy.420 = bf16[124,5,1,2048]{0,3,1,2:T(8,128)(2,1)S(1)} copy(bf16[124,5,1,2048]{3,0,2,1:T(8,128)(2,1)} %param.3) | data formatting | bytes 5079040 | tf_op args[1]
  83.6 2.6 %reshape.631 = bf16[256,5,1,4,8]{4,3,2,1,0:T(4,128)(2,1)} reshape(bf16[8,2,2560]{2,1,0:T(2,128)(2,1)S(1)} %all-to-all-done) | data formatting | bytes 163840
  86.2 1.8 copy.417
  88.0 0.2 copy.418
  88.2 0.3 convolution_bitcast_fusion
  88.5 0.2 reshape.625
  88.7 0.4 fusion.102
  89.1 0.1 pad_maximum_fusion.31
  89.2 0.1 copy.421
  89.3 0.7 maximum_multiply_fusion
  90.1 143.6 %all-reduce.2.cloned.1.call-done = f32[128,128]{0,1:T(8,128)} async-done(((f32[128,128]{0,1:T(8,128)}), f32[128,128]{0,1:T(8,128)}) %all-reduce.2.cloned.1.call-update) | async-done | bytes 65552 | tf_op jit(solution)/shard_map/psum | solution.py:106
  233.7 0.9 copy.422
  234.6 0.9 fusion.6
  235.5 11.7 %cholesky.18 = f32[128,128]{1,0:T(8,128)S(1)} custom-call(f32[128,128]{1,0:T(8,128)S(1)} %fusion.6), custom_call_target="Cholesky" | custom-call | tf_op jit(solution)/shard_map/jit(cholesky)/cholesky | solution.py:107
  247.2 0.6 compare_reduce_fusion
  247.9 0.7 select_bitcast_fusion
  248.5 0.7 copy.424
  (103 shorter events, 1.9 us)
Async XLA Ops:
  7.9 7.6 %collective-permute-start.1 = (bf16[5,1,8,256]{3,2,1,0:T(8,128)(2,1)S(1)}, bf16[5,1,8,256]{3,2,1,0:T(8,128)(2,1)S(1)}, u32[]{:S(2)}, u32[]{:S(2)}) collective-permute-start(bf16[5,1,8,256]{3,2,1,0:T(8,128)(2,1)S(1)} %convert_element_type.30), channel_id=1, source_target_pairs={{8,0},{16,8},{24,16},{32,24},{40,32},{48,40},{56,48},{64,56},{72,6... | collective-permute-start | bytes 61448 | tf_op jit(solution)/shard_map/ppermute | solution.py:21
  9.3 6.3 %collective-permute-start = (bf16[5,1,8,256]{3,2,1,0:T(8,128)(2,1)S(1)}, bf16[5,1,8,256]{3,2,1,0:T(8,128)(2,1)S(1)}, u32[]{:S(2)}, u32[]{:S(2)}) collective-permute-start(bf16[5,1,8,256]{3,2,1,0:T(8,128)(2,1)S(1)} %convert_element_type.30), channel_id=1, source_target_pairs={{0,8},{8,16},{16,24},{24,32},{32,40},{40,48},{48,56},{56,64},{64,7... | collective-permute-start | bytes 61448 | tf_op jit(solution)/shard_map/ppermute | solution.py:18
  11.7 30.4 %copy-start = (f32[5,1,8,256]{3,2,1,0:T(8,128)S(1)}, f32[5,1,8,256]{3,2,1,0:T(8,128)}, u32[]{:S(2)}) copy-start(f32[5,1,8,256]{3,2,1,0:T(8,128)} %param.2) | copy-start | bytes 122884
  15.7 6.0 %collective-permute-start.3 = (bf16[5,3,1,256]{3,1,2,0:T(4,128)(2,1)S(1)}, bf16[5,3,1,256]{3,1,2,0:T(4,128)(2,1)S(1)}, u32[]{:S(2)}, u32[]{:S(2)}) collective-permute-start(bf16[5,3,1,256]{3,1,2,0:T(4,128)(2,1)S(1)} %copy.427), channel_id=1, source_target_pairs={{1,0},{2,1},{3,2},{4,3},{5,4},{6,5},{7,6},{0,7},{9,8},{10,9},{11,1... | collective-permute-start | bytes 23048 | tf_op jit(solution)/shard_map/ppermute | solution.py:21
  20.8 6.1 %collective-permute-start.2 = (bf16[5,3,1,256]{3,1,2,0:T(4,128)(2,1)S(1)}, bf16[5,3,1,256]{3,1,2,0:T(4,128)(2,1)S(1)}, u32[]{:S(2)}, u32[]{:S(2)}) collective-permute-start(bf16[5,3,1,256]{3,1,2,0:T(4,128)(2,1)S(1)} %copy.426), channel_id=1, source_target_pairs={{0,1},{1,2},{2,3},{3,4},{4,5},{5,6},{6,7},{7,0},{8,9},{9,10},{10,1... | collective-permute-start | bytes 23048 | tf_op jit(solution)/shard_map/ppermute | solution.py:18
  28.2 5.7 %collective-permute-start.5 = (bf16[5,1,8,256]{3,2,0,1:T(8,128)(2,1)S(1)}, bf16[5,1,8,256]{3,2,0,1:T(8,128)(2,1)S(1)}, u32[]{:S(2)}, u32[]{:S(2)}) collective-permute-start(bf16[5,1,8,256]{3,2,0,1:T(8,128)(2,1)S(1)} %get-tuple-element.65), channel_id=1, source_target_pairs={{8,0},{16,8},{24,16},{32,24},{40,32},{48,40},{56,48},{64,56},{72,6... | collective-permute-start | bytes 61448 | tf_op jit(solution)/shard_map/ppermute | solution.py:21
  33.0 1.8 collective-permute-start.4
  34.9 4.2 %collective-permute-start.7 = (bf16[5,3,1,256]{3,1,2,0:T(4,128)(2,1)S(1)}, bf16[5,3,1,256]{3,1,2,0:T(4,128)(2,1)S(1)}, u32[]{:S(2)}, u32[]{:S(2)}) collective-permute-start(bf16[5,3,1,256]{3,1,2,0:T(4,128)(2,1)S(1)} %copy.383), channel_id=1, source_target_pairs={{1,0},{2,1},{3,2},{4,3},{5,4},{6,5},{7,6},{0,7},{9,8},{10,9},{11,1... | collective-permute-start | bytes 23048 | tf_op jit(solution)/shard_map/ppermute | solution.py:21
  35.6 6.1 %collective-permute-start.6 = (bf16[5,3,1,256]{3,1,2,0:T(4,128)(2,1)S(1)}, bf16[5,3,1,256]{3,1,2,0:T(4,128)(2,1)S(1)}, u32[]{:S(2)}, u32[]{:S(2)}) collective-permute-start(bf16[5,3,1,256]{3,1,2,0:T(4,128)(2,1)S(1)} %copy.382), channel_id=1, source_target_pairs={{0,1},{1,2},{2,3},{3,4},{4,5},{5,6},{6,7},{7,0},{8,9},{9,10},{10,1... | collective-permute-start | bytes 23048 | tf_op jit(solution)/shard_map/ppermute | solution.py:18
  42.3 7.0 %collective-permute-start.9 = (bf16[5,1,8,256]{3,2,0,1:T(8,128)(2,1)S(1)}, bf16[5,1,8,256]{3,2,0,1:T(8,128)(2,1)S(1)}, u32[]{:S(2)}, u32[]{:S(2)}) collective-permute-start(bf16[5,1,8,256]{3,2,0,1:T(8,128)(2,1)S(1)} %fusion.78), channel_id=1, source_target_pairs={{8,0},{16,8},{24,16},{32,24},{40,32},{48,40},{56,48},{64,56},{72,6... | collective-permute-start | bytes 61448 | tf_op jit(solution)/shard_map/ppermute | solution.py:21
  48.5 1.2 collective-permute-start.8
  49.7 4.1 %collective-permute-start.11 = (bf16[5,3,1,256]{3,1,2,0:T(4,128)(2,1)S(1)}, bf16[5,3,1,256]{3,1,2,0:T(4,128)(2,1)S(1)}, u32[]{:S(2)}, u32[]{:S(2)}) collective-permute-start(bf16[5,3,1,256]{3,1,2,0:T(4,128)(2,1)S(1)} %copy.395), channel_id=1, source_target_pairs={{1,0},{2,1},{3,2},{4,3},{5,4},{6,5},{7,6},{0,7},{9,8},{10,9},{11,1... | collective-permute-start | bytes 23048 | tf_op jit(solution)/shard_map/ppermute | solution.py:21
  49.8 6.2 %collective-permute-start.10 = (bf16[5,3,1,256]{3,1,2,0:T(4,128)(2,1)S(1)}, bf16[5,3,1,256]{3,1,2,0:T(4,128)(2,1)S(1)}, u32[]{:S(2)}, u32[]{:S(2)}) collective-permute-start(bf16[5,3,1,256]{3,1,2,0:T(4,128)(2,1)S(1)} %copy.394), channel_id=1, source_target_pairs={{0,1},{1,2},{2,3},{3,4},{4,5},{5,6},{6,7},{7,0},{8,9},{9,10},{10,1... | collective-permute-start | bytes 23048 | tf_op jit(solution)/shard_map/ppermute | solution.py:18
  56.4 6.3 %collective-permute-start.13 = (bf16[5,1,8,256]{3,2,0,1:T(8,128)(2,1)S(1)}, bf16[5,1,8,256]{3,2,0,1:T(8,128)(2,1)S(1)}, u32[]{:S(2)}, u32[]{:S(2)}) collective-permute-start(bf16[5,1,8,256]{3,2,0,1:T(8,128)(2,1)S(1)} %get-tuple-element.31), channel_id=1, source_target_pairs={{8,0},{16,8},{24,16},{32,24},{40,32},{48,40},{56,48},{64,56},{72,6... | collective-permute-start | bytes 61448 | tf_op jit(solution)/shard_map/ppermute | solution.py:21
  61.9 1.2 collective-permute-start.12
  63.1 4.1 %collective-permute-start.15 = (bf16[5,3,1,256]{3,1,2,0:T(4,128)(2,1)S(1)}, bf16[5,3,1,256]{3,1,2,0:T(4,128)(2,1)S(1)}, u32[]{:S(2)}, u32[]{:S(2)}) collective-permute-start(bf16[5,3,1,256]{3,1,2,0:T(4,128)(2,1)S(1)} %copy.406), channel_id=1, source_target_pairs={{1,0},{2,1},{3,2},{4,3},{5,4},{6,5},{7,6},{0,7},{9,8},{10,9},{11,1... | collective-permute-start | bytes 23048 | tf_op jit(solution)/shard_map/ppermute | solution.py:21
  63.2 6.2 %collective-permute-start.14 = (bf16[5,3,1,256]{3,1,2,0:T(4,128)(2,1)S(1)}, bf16[5,3,1,256]{3,1,2,0:T(4,128)(2,1)S(1)}, u32[]{:S(2)}, u32[]{:S(2)}) collective-permute-start(bf16[5,3,1,256]{3,1,2,0:T(4,128)(2,1)S(1)} %copy.405), channel_id=1, source_target_pairs={{0,1},{1,2},{2,3},{3,4},{4,5},{5,6},{6,7},{7,0},{8,9},{9,10},{10,1... | collective-permute-start | bytes 23048 | tf_op jit(solution)/shard_map/ppermute | solution.py:18
  73.3 10.3 %all-to-all-start = ((bf16[8,2,2560]{2,1,0:T(2,128)(2,1)}), bf16[8,2,2560]{2,1,0:T(2,128)(2,1)S(1)}, u32[]{:S(2)}, u32[]{:S(2)}) async-start(bf16[8,2,2560]{2,1,0:T(2,128)(2,1)} %reshape.630), calls=%async_computation | async-start | bytes 163840 | tf_op jit(solution)/shard_map/all_to_all | solution.py:90
  76.6 157.1 %all-reduce.2.cloned.1.call-start = ((), (), s32[]{:S(2)}) async-start(), calls=%async_computation.1 | async-start | bytes 131072 | tf_op jit(solution)/shard_map/psum | solution.py:106
Sparse Core Ops, SparseCore 0:
  90.2 143.4 all-reduce.1
where the time goes:
time: 257 us; the launch traced here: 256 us
  waiting for transfers between devices  162 us (63%)
  starting transfers between devices  37.3 us (15%)
  other arithmetic  21.4 us (8%)
  local copies, waits for them, and re-layouts  16.3 us (6%)
  between operations  14.7 us (6%)
  matrix products  4.08 us (2%)
    psum x1, waiting for transfers between devices, local(): gram_whole = lax.psum(gram_local, ('wide', 'narrow'))  144 us
    ppermute x8, starting transfers between devices, extended(): lax.ppermute(lax.slice_in_dim(block, 0, width, axis=dim), axis, backward)  23.8 us
    ppermute x8, waiting for transfers between devices, extended(): lax.ppermute(lax.slice_in_dim(block, block.shape[dim] - width, None, axis...  13.9 us
    another operation x3, other arithmetic, local(): factor = jnp.linalg.cholesky(gram_whole).T  12.4 us
    ppermute x8, starting transfers between devices, extended(): lax.ppermute(lax.slice_in_dim(block, block.shape[dim] - width, None, axis...  9.89 us
    unnamed x16, local copies, waits for them, and re-layouts  9.47 us
  transfers between devices with their start and end apart: 18, of which 14 were waited for; matrix products, arithmetic and copies ran while one was open for 5% of the time, Pallas kernels for 0%

commit v1 on v0

--- a/solution.py
+++ b/solution.py
@@ -2,6 +2,7 @@
 import jax.numpy as jnp
 from jax import lax
 from jax.sharding import PartitionSpec as P
+from jax.lax import psum
 
 STEPS = 2
 GAMMA = 1.4
@@ -103,7 +104,10 @@
         0,
     )
     gram_local = gram_local * inverse_cells
-    gram_whole = lax.psum(gram_local, ("wide", "narrow"))
+    spread_the_gates = lambda z_in, axis_id, which_axis: psum(
+        psum(z_in, axis_name=axis_id), axis_name=which_axis
+    )
+    gram_whole = spread_the_gates(gram_local, "wide", "narrow")
     factor = jnp.linalg.cholesky(gram_whole).T
     return (current, factor)
 

time: 257 us -> 312 us (1.21); the launches traced: 256 us -> 306 us
  waiting for transfers between devices: 162 us -> 213 us
    psum x1 -> x2, waiting for transfers between devices: 144 us -> 194 us  [the longest x1 110 us: local(): psum(z_in, axis_name=axis_id)]
  transfers between devices with their start and end apart: 18 -> 19, of which waited for: 14 -> 15; matrix products, arithmetic and copies ran while one was open for 5% -> 4% of each run, Pallas kernels for 0% -> 0%
where the time goes in v1:
time: 312 us; the launch traced here: 306 us
  waiting for transfers between devices  213 us (68%)
  starting transfers between devices  37.3 us (12%)
  other arithmetic  21.4 us (7%)
  local copies, waits for them, and re-layouts  16.3 us (5%)
  between operations  14.7 us (5%)
  matrix products  4.08 us (1%)
    psum x1, waiting for transfers between devices, local(): psum(z_in, axis_name=axis_id)  110 us
    psum x1, waiting for transfers between devices, local(): psum(psum(z_in, axis_name=axis_id), axis_name=which_axis)  84 us
    ppermute x8, starting transfers between devices, extended(): lax.ppermute(lax.slice_in_dim(block, 0, width, axis=dim), axis, backward)  23.8 us
    ppermute x8, waiting for transfers between devices, extended(): lax.ppermute(lax.slice_in_dim(block, block.shape[dim] - width, None, axis...  13.9 us
    another operation x3, other arithmetic, local(): factor = jnp.linalg.cholesky(gram_whole).T  12.4 us
    ppermute x8, starting transfers between devices, extended(): lax.ppermute(lax.slice_in_dim(block, block.shape[dim] - width, None, axis...  9.89 us
    unnamed x16, local copies, waits for them, and re-layouts  9.47 us
  transfers between devices with their start and end apart: 19, of which 15 were waited for; matrix products, arithmetic and copies ran while one was open for 4% of the time, Pallas kernels for 0%

profile of v1, /device:TPU:1, one launch (start us, length us, event | category | flops | bytes accessed | tf_op | source)
XLA Modules:
  0.0 306.3 jit_solution(13559636637448301448)
XLA Ops:
  7.2 0.8 convert_element_type.30
  7.9 1.4 collective-permute-start.1
  9.3 1.6 collective-permute-start
  11.0 0.7 constant_dynamic-update-slice_fusion.14
  11.7 0.8 constant_dynamic-update-slice_fusion.13
  12.4 0.7 constant_dynamic-update-slice_fusion.12
  13.1 0.8 constant_dynamic-update-slice_fusion.11
  13.9 0.7 constant_dynamic-update-slice_fusion.10
  14.6 0.9 fusion.98
  15.7 5.2 %collective-permute-start.3 = (bf16[5,3,1,256]{3,1,2,0:T(4,128)(2,1)S(1)}, bf16[5,3,1,256]{3,1,2,0:T(4,128)(2,1)S(1)}, u32[]{:S(2)}, u32[]{:S(2)}) collective-permute-start(bf16[5,3,1,256]{3,1,2,0:T(4,128)(2,1)S(1)} %copy.427), channel_id=1, source_target_pairs={{1,0},{2,1},{3,2},{4,3},{5,4},{6,5},{7,6},{0,7},{9,8},{10,9},{11,1... | collective-permute-start | bytes 23048 | tf_op jit(solution)/shard_map/ppermute | solution.py:22
  20.8 0.8 fusion.99
  21.7 5.3 %collective-permute-done.2 = bf16[5,3,1,256]{3,1,2,0:T(4,128)(2,1)S(1)} collective-permute-done((bf16[5,3,1,256]{3,1,2,0:T(4,128)(2,1)S(1)}, bf16[5,3,1,256]{3,1,2,0:T(4,128)(2,1)S(1)}, u32[]{:S(2)}, u32[]{:S(2)}) %collective-permute-start.2) | collective-permute-done | bytes 7712 | tf_op jit(solution)/shard_map/ppermute | solution.py:19
  27.3 0.9 fusion.83
  28.2 4.9 %collective-permute-start.5 = (bf16[5,1,8,256]{3,2,0,1:T(8,128)(2,1)S(1)}, bf16[5,1,8,256]{3,2,0,1:T(8,128)(2,1)S(1)}, u32[]{:S(2)}, u32[]{:S(2)}) collective-permute-start(bf16[5,1,8,256]{3,2,0,1:T(8,128)(2,1)S(1)} %get-tuple-element.65), channel_id=1, source_target_pairs={{8,0},{16,8},{24,16},{32,24},{40,32},{48,40},{56,48},{64,56},{72,6... | collective-permute-start | bytes 61448 | tf_op jit(solution)/shard_map/ppermute | solution.py:22
  33.2 0.1 fusion.94
  33.3 0.6 collective-permute-done.5
  33.9 1.0 collective-permute-done.4
  34.9 0.7 collective-permute-start.7
  35.6 2.3 collective-permute-start.6
  38.0 1.1 collective-permute-done.7
  39.1 2.6 collective-permute-done.6
  42.1 0.1 broadcast_multiply_fusion
  42.2 0.1 fusion.92
  42.3 6.1 %collective-permute-start.9 = (bf16[5,1,8,256]{3,2,0,1:T(8,128)(2,1)S(1)}, bf16[5,1,8,256]{3,2,0,1:T(8,128)(2,1)S(1)}, u32[]{:S(2)}, u32[]{:S(2)}) collective-permute-start(bf16[5,1,8,256]{3,2,0,1:T(8,128)(2,1)S(1)} %fusion.78), channel_id=1, source_target_pairs={{8,0},{16,8},{24,16},{32,24},{40,32},{48,40},{56,48},{64,56},{72,6... | collective-permute-start | bytes 61448 | tf_op jit(solution)/shard_map/ppermute | solution.py:22
  48.5 0.1 fusion.90
  48.7 0.6 collective-permute-done.9
  49.3 0.3 collective-permute-done.8
  49.7 0.1 collective-permute-start.11
  49.8 2.9 collective-permute-start.10
  52.8 1.0 collective-permute-done.11
  53.8 2.2 collective-permute-done.10
  56.3 0.1 fusion.80
  56.4 5.4 %collective-permute-start.13 = (bf16[5,1,8,256]{3,2,0,1:T(8,128)(2,1)S(1)}, bf16[5,1,8,256]{3,2,0,1:T(8,128)(2,1)S(1)}, u32[]{:S(2)}, u32[]{:S(2)}) collective-permute-start(bf16[5,1,8,256]{3,2,0,1:T(8,128)(2,1)S(1)} %get-tuple-element.31), channel_id=1, source_target_pairs={{8,0},{16,8},{24,16},{32,24},{40,32},{48,40},{56,48},{64,56},{72,6... | collective-permute-start | bytes 61448 | tf_op jit(solution)/shard_map/ppermute | solution.py:22
  62.0 0.1 fusion.86
  62.2 0.6 collective-permute-done.13
  62.7 0.3 collective-permute-done.12
  63.1 0.1 collective-permute-start.15
  63.2 2.9 collective-permute-start.14
  66.2 1.0 collective-permute-done.15
  67.2 2.2 collective-permute-done.14
  69.7 0.7 convert_bitcast_fusion
  70.5 0.7 copy.416
  71.2 2.1 reshape.630
  73.3 3.4 %all-to-all-start = ((bf16[8,2,2560]{2,1,0:T(2,128)(2,1)}), bf16[8,2,2560]{2,1,0:T(2,128)(2,1)S(1)}, u32[]{:S(2)}, u32[]{:S(2)}) async-start(bf16[8,2,2560]{2,1,0:T(2,128)(2,1)} %reshape.630), calls=%async_computation | async-start | bytes 163840 | tf_op jit(solution)/shard_map/all_to_all | solution.py:91
  76.6 0.2 all-reduce.3.cloned.1.call-start
  76.9 3.4 %fusion.2 = f32[124,124]{0,1:T(8,128)S(1)} fusion(bf16[124,5,1,2048]{3,0,2,1:T(8,128)(2,1)} %param.3), kind=kOutput, calls=%fused_computation.2 | convolution fusion | flops 314900480 | bytes 2601024 | tf_op jit(solution)/shard_map/dot_general | solution.py:81
  80.2 3.3 %copy.420 = bf16[124,5,1,2048]{0,3,1,2:T(8,128)(2,1)S(1)} copy(bf16[124,5,1,2048]{3,0,2,1:T(8,128)(2,1)} %param.3) | data formatting | bytes 5079040 | tf_op args[1]
  83.6 2.6 reshape.631
  86.2 1.8 copy.417
  88.0 0.2 copy.418
  88.2 0.3 convolution_bitcast_fusion
  88.5 0.2 reshape.625
  88.7 0.4 fusion.102
  89.1 0.1 pad_maximum_fusion.31
  89.2 0.1 copy.421
  89.3 0.7 maximum_multiply_fusion
  90.1 109.8 %all-reduce.3.cloned.1.call-done = f32[128,128]{0,1:T(8,128)} async-done(((f32[128,128]{0,1:T(8,128)}), f32[128,128]{0,1:T(8,128)}) %all-reduce.3.cloned.1.call-update) | async-done | bytes 65552 | tf_op jit(solution)/shard_map/psum | solution.py:108
  199.9 84.0 %all-reduce.5.cloned.1.call-done = f32[128,128]{0,1:T(8,128)} async-done(((f32[128,128]{0,1:T(8,128)}), f32[128,128]{0,1:T(8,128)}) %all-reduce.5.cloned.1.call-update) | async-done | bytes 65552 | tf_op jit(solution)/shard_map/psum | solution.py:107
  283.9 0.9 copy.422
  284.8 0.9 fusion.6
  285.7 11.7 %cholesky.18 = f32[128,128]{1,0:T(8,128)S(1)} custom-call(f32[128,128]{1,0:T(8,128)S(1)} %fusion.6), custom_call_target="Cholesky" | custom-call | tf_op jit(solution)/shard_map/jit(cholesky)/cholesky | solution.py:111
  297.4 0.6 compare_reduce_fusion
  298.1 0.7 select_bitcast_fusion
  298.7 0.7 copy.424
  (106 shorter events, 2.0 us)
Async XLA Ops:
  7.9 7.6 %collective-permute-start.1 = (bf16[5,1,8,256]{3,2,1,0:T(8,128)(2,1)S(1)}, bf16[5,1,8,256]{3,2,1,0:T(8,128)(2,1)S(1)}, u32[]{:S(2)}, u32[]{:S(2)}) collective-permute-start(bf16[5,1,8,256]{3,2,1,0:T(8,128)(2,1)S(1)} %convert_element_type.30), channel_id=1, source_target_pairs={{8,0},{16,8},{24,16},{32,24},{40,32},{48,40},{56,48},{64,56},{72,6... | collective-permute-start | bytes 61448 | tf_op jit(solution)/shard_map/ppermute | solution.py:22
  9.3 6.3 %collective-permute-start = (bf16[5,1,8,256]{3,2,1,0:T(8,128)(2,1)S(1)}, bf16[5,1,8,256]{3,2,1,0:T(8,128)(2,1)S(1)}, u32[]{:S(2)}, u32[]{:S(2)}) collective-permute-start(bf16[5,1,8,256]{3,2,1,0:T(8,128)(2,1)S(1)} %convert_element_type.30), channel_id=1, source_target_pairs={{0,8},{8,16},{16,24},{24,32},{32,40},{40,48},{48,56},{56,64},{64,7... | collective-permute-start | bytes 61448 | tf_op jit(solution)/shard_map/ppermute | solution.py:19
  11.7 30.4 %copy-start = (f32[5,1,8,256]{3,2,1,0:T(8,128)S(1)}, f32[5,1,8,256]{3,2,1,0:T(8,128)}, u32[]{:S(2)}) copy-start(f32[5,1,8,256]{3,2,1,0:T(8,128)} %param.2) | copy-start | bytes 122884
  15.7 6.0 %collective-permute-start.3 = (bf16[5,3,1,256]{3,1,2,0:T(4,128)(2,1)S(1)}, bf16[5,3,1,256]{3,1,2,0:T(4,128)(2,1)S(1)}, u32[]{:S(2)}, u32[]{:S(2)}) collective-permute-start(bf16[5,3,1,256]{3,1,2,0:T(4,128)(2,1)S(1)} %copy.427), channel_id=1, source_target_pairs={{1,0},{2,1},{3,2},{4,3},{5,4},{6,5},{7,6},{0,7},{9,8},{10,9},{11,1... | collective-permute-start | bytes 23048 | tf_op jit(solution)/shard_map/ppermute | solution.py:22
  20.8 6.1 %collective-permute-start.2 = (bf16[5,3,1,256]{3,1,2,0:T(4,128)(2,1)S(1)}, bf16[5,3,1,256]{3,1,2,0:T(4,128)(2,1)S(1)}, u32[]{:S(2)}, u32[]{:S(2)}) collective-permute-start(bf16[5,3,1,256]{3,1,2,0:T(4,128)(2,1)S(1)} %copy.426), channel_id=1, source_target_pairs={{0,1},{1,2},{2,3},{3,4},{4,5},{5,6},{6,7},{7,0},{8,9},{9,10},{10,1... | collective-permute-start | bytes 23048 | tf_op jit(solution)/shard_map/ppermute | solution.py:19
  28.2 5.7 %collective-permute-start.5 = (bf16[5,1,8,256]{3,2,0,1:T(8,128)(2,1)S(1)}, bf16[5,1,8,256]{3,2,0,1:T(8,128)(2,1)S(1)}, u32[]{:S(2)}, u32[]{:S(2)}) collective-permute-start(bf16[5,1,8,256]{3,2,0,1:T(8,128)(2,1)S(1)} %get-tuple-element.65), channel_id=1, source_target_pairs={{8,0},{16,8},{24,16},{32,24},{40,32},{48,40},{56,48},{64,56},{72,6... | collective-permute-start | bytes 61448 | tf_op jit(solution)/shard_map/ppermute | solution.py:22
  33.0 1.8 collective-permute-start.4
  34.9 4.2 %collective-permute-start.7 = (bf16[5,3,1,256]{3,1,2,0:T(4,128)(2,1)S(1)}, bf16[5,3,1,256]{3,1,2,0:T(4,128)(2,1)S(1)}, u32[]{:S(2)}, u32[]{:S(2)}) collective-permute-start(bf16[5,3,1,256]{3,1,2,0:T(4,128)(2,1)S(1)} %copy.383), channel_id=1, source_target_pairs={{1,0},{2,1},{3,2},{4,3},{5,4},{6,5},{7,6},{0,7},{9,8},{10,9},{11,1... | collective-permute-start | bytes 23048 | tf_op jit(solution)/shard_map/ppermute | solution.py:22
  35.6 6.1 %collective-permute-start.6 = (bf16[5,3,1,256]{3,1,2,0:T(4,128)(2,1)S(1)}, bf16[5,3,1,256]{3,1,2,0:T(4,128)(2,1)S(1)}, u32[]{:S(2)}, u32[]{:S(2)}) collective-permute-start(bf16[5,3,1,256]{3,1,2,0:T(4,128)(2,1)S(1)} %copy.382), channel_id=1, source_target_pairs={{0,1},{1,2},{2,3},{3,4},{4,5},{5,6},{6,7},{7,0},{8,9},{9,10},{10,1... | collective-permute-start | bytes 23048 | tf_op jit(solution)/shard_map/ppermute | solution.py:19
  42.3 7.0 %collective-permute-start.9 = (bf16[5,1,8,256]{3,2,0,1:T(8,128)(2,1)S(1)}, bf16[5,1,8,256]{3,2,0,1:T(8,128)(2,1)S(1)}, u32[]{:S(2)}, u32[]{:S(2)}) collective-permute-start(bf16[5,1,8,256]{3,2,0,1:T(8,128)(2,1)S(1)} %fusion.78), channel_id=1, source_target_pairs={{8,0},{16,8},{24,16},{32,24},{40,32},{48,40},{56,48},{64,56},{72,6... | collective-permute-start | bytes 61448 | tf_op jit(solution)/shard_map/ppermute | solution.py:22
  48.5 1.2 collective-permute-start.8
  49.7 4.1 %collective-permute-start.11 = (bf16[5,3,1,256]{3,1,2,0:T(4,128)(2,1)S(1)}, bf16[5,3,1,256]{3,1,2,0:T(4,128)(2,1)S(1)}, u32[]{:S(2)}, u32[]{:S(2)}) collective-permute-start(bf16[5,3,1,256]{3,1,2,0:T(4,128)(2,1)S(1)} %copy.395), channel_id=1, source_target_pairs={{1,0},{2,1},{3,2},{4,3},{5,4},{6,5},{7,6},{0,7},{9,8},{10,9},{11,1... | collective-permute-start | bytes 23048 | tf_op jit(solution)/shard_map/ppermute | solution.py:22
  49.8 6.2 %collective-permute-start.10 = (bf16[5,3,1,256]{3,1,2,0:T(4,128)(2,1)S(1)}, bf16[5,3,1,256]{3,1,2,0:T(4,128)(2,1)S(1)}, u32[]{:S(2)}, u32[]{:S(2)}) collective-permute-start(bf16[5,3,1,256]{3,1,2,0:T(4,128)(2,1)S(1)} %copy.394), channel_id=1, source_target_pairs={{0,1},{1,2},{2,3},{3,4},{4,5},{5,6},{6,7},{7,0},{8,9},{9,10},{10,1... | collective-permute-start | bytes 23048 | tf_op jit(solution)/shard_map/ppermute | solution.py:19
  56.4 6.3 %collective-permute-start.13 = (bf16[5,1,8,256]{3,2,0,1:T(8,128)(2,1)S(1)}, bf16[5,1,8,256]{3,2,0,1:T(8,128)(2,1)S(1)}, u32[]{:S(2)}, u32[]{:S(2)}) collective-permute-start(bf16[5,1,8,256]{3,2,0,1:T(8,128)(2,1)S(1)} %get-tuple-element.31), channel_id=1, source_target_pairs={{8,0},{16,8},{24,16},{32,24},{40,32},{48,40},{56,48},{64,56},{72,6... | collective-permute-start | bytes 61448 | tf_op jit(solution)/shard_map/ppermute | solution.py:22
  61.9 1.2 collective-permute-start.12
  63.1 4.1 %collective-permute-start.15 = (bf16[5,3,1,256]{3,1,2,0:T(4,128)(2,1)S(1)}, bf16[5,3,1,256]{3,1,2,0:T(4,128)(2,1)S(1)}, u32[]{:S(2)}, u32[]{:S(2)}) collective-permute-start(bf16[5,3,1,256]{3,1,2,0:T(4,128)(2,1)S(1)} %copy.406), channel_id=1, source_target_pairs={{1,0},{2,1},{3,2},{4,3},{5,4},{6,5},{7,6},{0,7},{9,8},{10,9},{11,1... | collective-permute-start | bytes 23048 | tf_op jit(solution)/shard_map/ppermute | solution.py:22
  63.2 6.2 %collective-permute-start.14 = (bf16[5,3,1,256]{3,1,2,0:T(4,128)(2,1)S(1)}, bf16[5,3,1,256]{3,1,2,0:T(4,128)(2,1)S(1)}, u32[]{:S(2)}, u32[]{:S(2)}) collective-permute-start(bf16[5,3,1,256]{3,1,2,0:T(4,128)(2,1)S(1)} %copy.405), channel_id=1, source_target_pairs={{0,1},{1,2},{2,3},{3,4},{4,5},{5,6},{6,7},{7,0},{8,9},{9,10},{10,1... | collective-permute-start | bytes 23048 | tf_op jit(solution)/shard_map/ppermute | solution.py:19
  73.3 10.3 %all-to-all-start = ((bf16[8,2,2560]{2,1,0:T(2,128)(2,1)}), bf16[8,2,2560]{2,1,0:T(2,128)(2,1)S(1)}, u32[]{:S(2)}, u32[]{:S(2)}) async-start(bf16[8,2,2560]{2,1,0:T(2,128)(2,1)} %reshape.630), calls=%async_computation | async-start | bytes 163840 | tf_op jit(solution)/shard_map/all_to_all | solution.py:91
  76.6 123.3 %all-reduce.3.cloned.1.call-start = ((), (), s32[]{:S(2)}) async-start(), calls=%async_computation.1 | async-start | bytes 131072 | tf_op jit(solution)/shard_map/psum | solution.py:108
  90.1 193.8 %all-reduce.5.cloned.1.call-start = ((), (), s32[]{:S(2)}) async-start(), calls=%async_computation.2 | async-start | bytes 131072 | tf_op jit(solution)/shard_map/psum | solution.py:107
Sparse Core Ops, SparseCore 0:
  90.2 109.6 all-reduce.2
  202.4 81.4 all-reduce.4
